TPU v7x, 256 devices: a whole 4x4x8 slice. The times are simulated.
256 devices in a mesh: frame: 16 (over y, z_hi, core), row: 16 (over x, z_lo).
Axes of the slice: x: 4, y: 4, z: 8 (z_hi: 2, z_lo: 4; z = z_hi * 4 + z_lo), core: 2. Of those that a mesh axis runs over, the one named last changes fastest.
Arguments:
- spatial_q: bfloat16 [32, 128, 32, 1152], P('frame', 'row'), may hold values from -10.5 to 10.5
- spatial_k: bfloat16 [32, 128, 32, 1152], P('frame', 'row'), may hold values from -10.5 to 10.5
- spatial_v: bfloat16 [32, 128, 32, 1152], P('frame', 'row'), may hold values from -6 to 6
- residual: bfloat16 [32, 128, 32, 1152], P('frame', 'row'), may hold values from -6 to 6
- neighbour_list: int32 [64, 6], P('row'), may hold values from 0 to 15, as said below
- block_mask: int32 [8, 8], replicated, may hold values from 0 to 1, as said below
- out_weight: bfloat16 [1152, 1152], P('frame'), may hold values from -0.1875 to 0.1875
- qkv_weight: bfloat16 [1152, 3456], P('frame'), may hold values from -1.4799 to 1.4799
- pos_embed: float32 [32, 1152], P('frame'), may hold values from -150.5 to 150.5
- mod_shift: float32 [1152], replicated, may hold values from -2 to 2
- mod_scale: float32 [1152], replicated, may hold values from -2 to 2
Outputs:
- temporal_mix: bfloat16 [32, 128, 32, 1152], P('frame', 'row')
Inputs may be any that keep to these rules, and one draw needn't show every extreme that they name: `neighbour_list`: each row holds 6 different tiles of its own clip: slot 0 is the row's own tile; every other lies at most one tile row and at most two tile columns away from it, inside the grid of 16 tiles. `block_mask`: entry (i, j) is 1 where i == j and 0 where j > i.
All inputs are finite; a program needn't handle non-finite values.
Results may differ from a plain program's by a relative error of at most 0.0056.
The roundings to bfloat16 on the way count: a program that leaves them out, or rounds other values in their place, can miss the bound.
Values may be sent and summed in bfloat16 or wider, within the bound.
No kernel may reach another device: no remote copies, remote signals or barrier semaphores. Data moves between devices by JAX's collectives and lax.ppermute only.
A program may use at most 128 MiB of HBM per device.

v0:
```python
import math

import jax
import jax.numpy as jnp
from jax import lax
from jax.experimental import pallas as pl
from jax.experimental.pallas import tpu as pltpu
from jax.sharding import PartitionSpec as P


HEADS = 16
TILE = 8
SLOTS = 6
TILES_WIDE = 4
D = 1152
HEAD = D // HEADS
EPS = 1e-06
ROW_AXIS = ("x", "zl")
FRAME_AXIS = ("y", "zh", "core")
PEERS = 16
PAIRS = HEADS // 2
WINDOW = 256
LANES = 128
NT = (((1,), (1,)), ((), ()))
RATE = (1.0 / math.sqrt(HEAD)) * math.log2(math.e)


def pair_masks(pair):
    lane = lax.broadcasted_iota(jnp.int32, (1, WINDOW), 1) + LANES * pair
    first = (lane >= 2 * pair * HEAD) & (lane < (2 * pair + 1) * HEAD)
    second = (lane >= (2 * pair + 1) * HEAD) & (lane < (2 * pair + 2) * HEAD)
    return first, second


def soft(scores):
    peak = jnp.max(scores, axis=-1, keepdims=True)
    powers = jnp.exp2((scores - peak) * RATE)
    total = jnp.sum(powers, axis=-1, keepdims=True)
    return (powers * (1.0 / total)).astype(jnp.bfloat16)


def attend(window_of, bias):
    carried = None
    for pair in range(PAIRS):
        first, second = pair_masks(pair)
        queries, keys, values = window_of(pair)
        rows = queries.shape[0]
        zero = jnp.zeros_like(queries)
        both = jnp.concatenate(
            [jnp.where(first, queries, zero), jnp.where(second, queries, zero)], axis=0
        )
        scores = lax.dot_general(both, keys, NT, preferred_element_type=jnp.float32)
        if bias is not None:
            scores = scores + jnp.concatenate([bias, bias], axis=0)
        weights = soft(scores)
        out = jnp.dot(weights, values, preferred_element_type=jnp.float32)
        out = jnp.where(first, out[:rows], jnp.where(second, out[rows:], 0.0))
        low, high = out[:, :LANES], out[:, LANES:]
        yield pair, low if carried is None else low + carried
        carried = high
    yield PAIRS, carried


def spatial_kernel(
    ids,
    q_ref,
    k_own,
    v_own,
    low,
    high,
    res_ref,
    w_ref,
    pos_ref,
    shift_ref,
    scale_ref,
    out_ref,
    qt,
    kt,
    vt,
    kw,
    vw,
    heads,
    acc,
):
    size = TILE * TILE

    def tile_up(i, _):
        for dst, base, src in (
            (qt, 0, q_ref),
            (kt, 0, low.at[0]),
            (kt, 4, k_own),
            (kt, 8, high.at[0]),
            (vt, 0, low.at[1]),
            (vt, 4, v_own),
            (vt, 8, high.at[1]),
        ):
            rows = src[pl.ds(2 * i, 2)].astype(jnp.float32)
            for c in range(TILES_WIDE):
                part = rows[:, c * TILE : (c + 1) * TILE, :].reshape(2 * TILE, D)
                dst[base + c, pl.ds(pl.multiple_of(16 * i, 16), 16), :] = part.astype(jnp.bfloat16)
        return 0

    lax.fori_loop(0, TILE // 2, tile_up, 0)

    def column(w, _):
        for slot in range(SLOTS):
            tile = ids[w * SLOTS + slot]
            kw[slot * size : (slot + 1) * size, :] = kt[tile]
            vw[slot * size : (slot + 1) * size, :] = vt[tile]

        def window_of(pair):
            lanes = slice(LANES * pair, LANES * pair + WINDOW)
            return qt[w, :, lanes], kw[:, lanes], vw[:, lanes]

        for block, value in attend(window_of, None):
            heads[pl.ds(pl.multiple_of(w * size, size), size), block * LANES : (block + 1) * LANES] = (
                value.astype(jnp.bfloat16)
            )
        return 0

    lax.fori_loop(0, TILES_WIDE, column, 0)
    acc[...] = jnp.dot(heads[...], w_ref[...], preferred_element_type=jnp.float32)

    def finish(i, _):
        added = jnp.concatenate(
            [
                acc[pl.ds(pl.multiple_of(c * size + 16 * i, 16), 16), :].reshape(2, TILE, D)
                for c in range(TILES_WIDE)
            ],
            axis=1,
        ).reshape(2 * TILES_WIDE * TILE, D)
        left = res_ref[pl.ds(2 * i, 2)].astype(jnp.float32).reshape(2 * TILES_WIDE * TILE, D)
        mixed = (left + added).astype(jnp.bfloat16).astype(jnp.float32)
        shifted = mixed + pos_ref[...]
        average = jnp.mean(shifted, axis=-1, keepdims=True)
        centred = shifted - average
        spread = jnp.mean(centred * centred, axis=-1, keepdims=True)
        normed = centred * lax.rsqrt(spread + EPS) * (1.0 + scale_ref[...]) + shift_ref[...]
        out_ref[pl.ds(2 * i, 2)] = normed.reshape(2, TILES_WIDE * TILE, D).astype(jnp.bfloat16)
        return 0

    lax.fori_loop(0, TILE // 2, finish, 0)


def spatial(frame, ids, q, k, v, low, high, residual, weight, pos, shift, scale):
    height, breadth = q.shape[1:3]
    own = pl.BlockSpec((pl.squeezed, height, breadth, D), lambda g, s: (frame, 0, 0, 0))
    halo = pl.BlockSpec((2, height, breadth, D), lambda g, s: (0, 0, 0, 0))
    row = pl.BlockSpec((1, D), lambda g, s: (0, 0))
    tokens = height * breadth
    bf16 = jnp.bfloat16
    return pl.pallas_call(
        spatial_kernel,
        out_shape=jax.ShapeDtypeStruct((height, breadth, D), bf16),
        grid_spec=pltpu.PrefetchScalarGridSpec(
            num_scalar_prefetch=1,
            grid=(1,),
            in_specs=[
                own,
                own,
                own,
                halo,
                halo,
                own,
                pl.BlockSpec((D, D), lambda g, s: (0, 0)),
                row,
                row,
                row,
            ],
            out_specs=pl.BlockSpec((height, breadth, D), lambda g, s: (0, 0, 0)),
            scratch_shapes=[
                pltpu.VMEM((4, 64, D), bf16),
                pltpu.VMEM((12, 64, D), bf16),
                pltpu.VMEM((12, 64, D), bf16),
                pltpu.VMEM((384, D), bf16),
                pltpu.VMEM((384, D), bf16),
                pltpu.VMEM((tokens, D), bf16),
                pltpu.VMEM((tokens, D), jnp.float32),
            ],
        ),
        compiler_params=pltpu.CompilerParams(vmem_limit_bytes=56 << 20),
        name="spatial",
    )(ids, q, k, v, low, high, residual, weight, pos, shift, scale)


def temporal_kernel(even_ref, odd_ref, w_ref, mask_ref, out_ref, xs, proj, done):
    per_frame = even_ref.shape[0]
    spots = done.shape[1]
    peers = per_frame // spots
    half = peers * TILE
    rows = 2 * half
    blocks = mask_ref.shape[0]
    r = lax.broadcasted_iota(jnp.int32, (rows, rows), 0)
    c = lax.broadcasted_iota(jnp.int32, (rows, rows), 1)
    near = (lax.broadcasted_iota(jnp.int32, (rows, blocks), 0) % half) // (half // blocks)
    spread = (near == lax.broadcasted_iota(jnp.int32, (rows, blocks), 1)).astype(jnp.bfloat16)
    reach = jnp.dot(spread, mask_ref[...], preferred_element_type=jnp.float32).astype(jnp.bfloat16)
    allowed = lax.dot_general(reach, spread, NT, preferred_element_type=jnp.float32)
    bias = jnp.where((allowed > 0.5) & (r % TILE == c % TILE), 0.0, -1e30)
    for f, src in enumerate((even_ref, odd_ref)):
        whole = src[...].astype(jnp.float32).reshape(peers, spots, D)
        for g in range(spots // TILE):
            part = whole[:, g * TILE : (g + 1) * TILE, :].reshape(half, D)
            xs[g * rows + f * half : g * rows + (f + 1) * half, :] = part.astype(jnp.bfloat16)
    proj[...] = jnp.dot(xs[...], w_ref[...], preferred_element_type=jnp.float32).astype(jnp.bfloat16)
    for g in range(spots // TILE):

        def window_of(pair):
            lane = LANES * pair
            here = slice(g * rows, (g + 1) * rows)
            return tuple(proj[here, base + lane : base + lane + WINDOW] for base in (0, D, 2 * D))

        for block, value in attend(window_of, bias):
            done[:, g * TILE : (g + 1) * TILE, block * LANES : (block + 1) * LANES] = value.reshape(
                2 * peers, TILE, LANES
            )
    for f in range(2):
        out_ref[f] = done[f * peers : (f + 1) * peers].reshape(per_frame, D).astype(jnp.bfloat16)


def temporal(even, odd, weight, mask):
    per_frame, _ = even.shape
    peers = PEERS
    spots = per_frame // peers
    return pl.pallas_call(
        temporal_kernel,
        out_shape=jax.ShapeDtypeStruct((2, per_frame, D), jnp.bfloat16),
        scratch_shapes=[
            pltpu.VMEM((2 * per_frame, D), jnp.bfloat16),
            pltpu.VMEM((2 * per_frame, 3 * D), jnp.bfloat16),
            pltpu.VMEM((2 * peers, spots, D), jnp.float32),
        ],
        compiler_params=pltpu.CompilerParams(vmem_limit_bytes=56 << 20),
        name="temporal",
    )(even, odd, weight, mask)


def mirrored(weight):
    return lax.ppermute(weight, ("zh", "zl"), [(i, 7 - i) for i in range(8)])


def gathered(weight, other):
    first = lax.axis_index("zh") == 0
    pair = jnp.stack((jnp.where(first, weight, other), jnp.where(first, other, weight)), 0)
    full = lax.all_gather(pair, ("y", "core"), axis=0, tiled=False)
    rows, cols = weight.shape
    full = full.reshape(4, 2, 2, rows, cols)
    return jnp.transpose(full, (0, 2, 1, 3, 4)).reshape(16 * rows, cols)


def local(
    spatial_q,
    spatial_k,
    spatial_v,
    residual,
    neighbour_list,
    block_mask,
    out_weight,
    qkv_weight,
    pos_embed,
    mod_shift,
    mod_scale,
):
    frames_here, height, breadth, channels = spatial_q.shape
    spots = height * breadth
    count = lax.axis_size(ROW_AXIS)
    down = [(i, (i + 1) % count) for i in range(count) if (i + 1) % 4 != 3]
    up = [(target, source) for source, target in down]
    moved = []
    for f in range(frames_here):
        both = jnp.stack((spatial_k[f], spatial_v[f]), 0)
        low = lax.ppermute(both, ROW_AXIS, down)
        high = lax.ppermute(both, ROW_AXIS, up)
        moved.append((low, high))
    w_out = gathered(out_weight, mirrored(out_weight))
    w_qkv = gathered(qkv_weight, mirrored(qkv_weight))
    tile_row_here = (lax.axis_index(ROW_AXIS) + 1) % 4
    ids = (
        (neighbour_list // TILES_WIDE - tile_row_here + 1) * TILES_WIDE
        + neighbour_list % TILES_WIDE
    ).reshape(-1)
    shift = mod_shift.reshape(1, channels)
    scale = mod_scale.reshape(1, channels)
    arrived = []
    for f in range(frames_here):
        low, high = moved[f]
        if f == frames_here - 1:
            low, w_qkv = lax.optimization_barrier((low, w_qkv))
        normed = spatial(
            f,
            ids,
            spatial_q,
            spatial_k,
            spatial_v,
            low,
            high,
            residual,
            w_out,
            pos_embed[f].reshape(1, channels),
            shift,
            scale,
        ).reshape(spots, channels)
        arrived.append(
            lax.all_to_all(normed, FRAME_AXIS, split_axis=0, concat_axis=0, tiled=True)
        )
    mask = block_mask.astype(jnp.bfloat16)
    done = temporal(arrived[0], arrived[1], w_qkv, mask)
    returned = lax.all_to_all(done, FRAME_AXIS, split_axis=1, concat_axis=1, tiled=True)
    return returned.reshape(frames_here, height, breadth, channels)


def solution(mesh):
    fine = jax.sharding.Mesh(mesh.devices.reshape(4, 2, 2, 4, 4), ("y", "zh", "core", "x", "zl"))
    tokens = P(FRAME_AXIS, ROW_AXIS, None, None)

    return jax.shard_map(
        local,
        mesh=fine,
        in_specs=(
            tokens,
            tokens,
            tokens,
            tokens,
            P(ROW_AXIS, None),
            P(),
            P(FRAME_AXIS, None),
            P(FRAME_AXIS, None),
            P(FRAME_AXIS, None),
            P(),
            P(),
        ),
        out_specs=tokens,
        check_vma=False,
    )
```

profile of v0, /device:TPU:38, one launch (start us, length us, event | category | flops | bytes accessed | tf_op | source)
XLA Modules:
  0.0 262.5 jit_solution(14108564018819742701)
XLA Ops:
  6.5 5.8 %collective-permute-start.2 = (bf16[72,1152]{1,0:T(8,128)(2,1)}, bf16[72,1152]{1,0:T(8,128)(2,1)S(1)}, u32[]{:S(2)}, u32[]{:S(2)}) collective-permute-start(bf16[72,1152]{1,0:T(8,128)(2,1)} %param.17), channel_id=1, source_target_pairs={{0,35},{1,34},{2,33},{3,32},{32,3},{33,2},{34,1},{35,0},{4,39},{5,... | collective-permute-start | bytes 497672 | tf_op jit(solution)/shard_map/ppermute | solution.py:239
  12.4 4.5 %collective-permute-done.2 = bf16[72,1152]{1,0:T(8,128)(2,1)S(1)} collective-permute-done((bf16[72,1152]{1,0:T(8,128)(2,1)}, bf16[72,1152]{1,0:T(8,128)(2,1)S(1)}, u32[]{:S(2)}, u32[]{:S(2)}) %collective-permute-start.2) | collective-permute-done | bytes 165920 | tf_op jit(solution)/shard_map/ppermute | solution.py:239
  16.9 0.9 select_bitcast_fusion.3
  17.9 0.7 pad_maximum_fusion.3
  18.7 4.8 %collective-permute-start.4 = (bf16[72,3456]{1,0:T(8,128)(2,1)S(1)}, bf16[72,3456]{1,0:T(8,128)(2,1)S(1)}, u32[]{:S(2)}, u32[]{:S(2)}) collective-permute-start(bf16[72,3456]{1,0:T(8,128)(2,1)S(1)} %copy-done.6), channel_id=1, source_target_pairs={{0,35},{1,34},{2,33},{3,32},{32,3},{33,2},{34,1},{35,0},{4,39},{5,... | collective-permute-start | bytes 1493000 | tf_op jit(solution)/shard_map/ppermute | solution.py:239
  23.6 10.8 %collective-permute-done.4 = bf16[72,3456]{1,0:T(8,128)(2,1)S(1)} collective-permute-done((bf16[72,3456]{1,0:T(8,128)(2,1)S(1)}, bf16[72,3456]{1,0:T(8,128)(2,1)S(1)}, u32[]{:S(2)}, u32[]{:S(2)}) %collective-permute-start.4) | collective-permute-done | bytes 497696 | tf_op jit(solution)/shard_map/ppermute | solution.py:239
  34.5 1.1 pad_maximum_fusion.2
  36.8 1.1 pad_maximum_fusion
  37.9 2.9 %collective-permute-start = (bf16[2,8,32,1152]{3,2,1,0:T(8,128)(2,1)}, bf16[2,8,32,1152]{3,2,1,0:T(8,128)(2,1)}, u32[]{:S(2)}, u32[]{:S(2)}) collective-permute-start(bf16[2,8,32,1152]{3,2,1,0:T(8,128)(2,1)} %pad_maximum_fusion), channel_id=1, source_target_pairs={{0,1},{1,2},{3,4},{4,5},{5,6},{7,8},{8,9},{9,10},{11,12},{12,13},{... | collective-permute-start | bytes 3538952 | tf_op jit(solution)/shard_map/ppermute | solution.py:272
  40.8 12.0 %collective-permute-start.1 = (bf16[2,8,32,1152]{3,2,1,0:T(8,128)(2,1)}, bf16[2,8,32,1152]{3,2,1,0:T(8,128)(2,1)}, u32[]{:S(2)}, u32[]{:S(2)}) collective-permute-start(bf16[2,8,32,1152]{3,2,1,0:T(8,128)(2,1)} %pad_maximum_fusion), channel_id=1, source_target_pairs={{1,0},{2,1},{4,3},{5,4},{6,5},{8,7},{9,8},{10,9},{12,11},{13,12},{... | collective-permute-start | bytes 3538952 | tf_op jit(solution)/shard_map/ppermute | solution.py:273
  52.9 1.1 pad_maximum_fusion.1
  54.0 1.9 collective-permute-start.3
  56.0 7.6 %collective-permute-start.5 = (bf16[2,8,32,1152]{3,2,1,0:T(8,128)(2,1)}, bf16[2,8,32,1152]{3,2,1,0:T(8,128)(2,1)S(1)}, u32[]{:S(2)}, u32[]{:S(2)}) collective-permute-start(bf16[2,8,32,1152]{3,2,1,0:T(8,128)(2,1)} %pad_maximum_fusion.1), channel_id=1, source_target_pairs={{1,0},{2,1},{4,3},{5,4},{6,5},{8,7},{9,8},{10,9},{12,11},{13,12},{... | collective-permute-start | bytes 3538952 | tf_op jit(solution)/shard_map/ppermute | solution.py:273
  63.6 0.6 fusion.8
  64.2 0.7 reshape.32.ids
  64.9 0.6 reshape.35.shift_ref
  65.5 0.6 reshape.36.scale_ref
  66.1 4.0 %copy.14 = bf16[4,2,2,72,1152]{4,3,1,2,0:T(8,128)(2,1)} copy(bf16[4,2,2,72,1152]{4,3,2,1,0:T(8,128)(2,1)} %bitcast.26) | data formatting | bytes 5308416 | tf_op jit(solution)/shard_map/reshape | solution.py:247
  70.1 7.9 %collective-permute-done.low = bf16[2,8,32,1152]{3,2,1,0:T(8,128)(2,1)} collective-permute-done((bf16[2,8,32,1152]{3,2,1,0:T(8,128)(2,1)}, bf16[2,8,32,1152]{3,2,1,0:T(8,128)(2,1)}, u32[]{:S(2)}, u32[]{:S(2)}) %collective-permute-start) | collective-permute-done | bytes 1179680 | tf_op jit(solution)/shard_map/ppermute | solution.py:272
  78.0 51.1 %collective-permute-done.1.high = bf16[2,8,32,1152]{3,2,1,0:T(8,128)(2,1)} collective-permute-done((bf16[2,8,32,1152]{3,2,1,0:T(8,128)(2,1)}, bf16[2,8,32,1152]{3,2,1,0:T(8,128)(2,1)}, u32[]{:S(2)}, u32[]{:S(2)}) %collective-permute-start.1) | collective-permute-done | bytes 1179680 | tf_op jit(solution)/shard_map/ppermute | solution.py:273
  129.2 19.9 %spatial.2 = bf16[8,32,1152]{2,1,0:T(8,128)(2,1)} custom-call(s32[24]{0:T(128)} %reshape.32.ids, bf16[2,8,32,1152]{3,2,1,0:T(8,128)(2,1)} %q_ref.3, bf16[2,8,32,1152]{3,2,1,0:T(8,128)(2,1)} %k_own.3, bf16[2,8,32,1152]{3,2,1,0:T(8,128)(2,1)} %v_own.3, bf16[2,8,32,1152]{3,2,1,0:T(8,128)(2,1)} %collective-permute-done.low, ...), custom_call_target="tpu_custom_call" | custom-call | tf_op jit(solution)/shard_map/spatial/pallas_call | solution.py:152
  149.0 8.9 %all-to-all-start = ((bf16[16,16,1152]{2,1,0:T(8,128)(2,1)}), bf16[16,16,1152]{2,1,0:T(8,128)(2,1)S(1)}, u32[]{:S(2)}, u32[]{:S(2)}) async-start(bf16[16,16,1152]{2,1,0:T(8,128)(2,1)} %bitcast.28), calls=%async_computation | async-start | bytes 1179648 | tf_op jit(solution)/shard_map/all_to_all | solution.py:304
  157.9 6.9 %copy.15 = bf16[4,2,2,72,3456]{4,3,1,2,0:T(8,128)(2,1)} copy(bf16[4,2,2,72,3456]{4,3,2,1,0:T(8,128)(2,1)} %bitcast.24) | data formatting | bytes 15925248 | tf_op jit(solution)/shard_map/reshape | solution.py:247
  164.8 1.0 copy-done.4
  166.2 19.9 %spatial.3 = bf16[8,32,1152]{2,1,0:T(8,128)(2,1)} custom-call(s32[24]{0:T(128)} %reshape.32.ids, bf16[2,8,32,1152]{3,2,1,0:T(8,128)(2,1)} %q_ref.3, bf16[2,8,32,1152]{3,2,1,0:T(8,128)(2,1)} %k_own.3, bf16[2,8,32,1152]{3,2,1,0:T(8,128)(2,1)} %v_own.3, bf16[2,8,32,1152]{3,2,1,0:T(8,128)(2,1)} %copy-done.4, bf16[2,8,32,1152]{3,2,1,0:T(8,128)(2,1)} %copy-done.5, ...), custom_call_target="tpu_custom_call" | custom-call | tf_op jit(solution)/shard_map/spatial/pallas_call | solution.py:152
  186.1 9.6 %all-to-all-start.1 = ((bf16[16,16,1152]{2,1,0:T(8,128)(2,1)}), bf16[16,16,1152]{2,1,0:T(8,128)(2,1)S(1)}, u32[]{:S(2)}, u32[]{:S(2)}) async-start(bf16[16,16,1152]{2,1,0:T(8,128)(2,1)} %bitcast.29), calls=%async_computation.1 | async-start | bytes 1179648 | tf_op jit(solution)/shard_map/all_to_all | solution.py:304
  196.3 14.8 %all-to-all-done.1 = bf16[16,16,1152]{2,1,0:T(8,128)(2,1)S(1)} async-done(((bf16[16,16,1152]{2,1,0:T(8,128)(2,1)}), bf16[16,16,1152]{2,1,0:T(8,128)(2,1)S(1)}, u32[]{:S(2)}, u32[]{:S(2)}) %all-to-all-start.1) | async-done | bytes 589856 | tf_op jit(solution)/shard_map/all_to_all | solution.py:304
  211.2 0.8 copy-done.3
  212.0 14.0 %temporal.1 = bf16[2,256,1152]{2,1,0:T(8,128)(2,1)} custom-call(bf16[256,1152]{1,0:T(8,128)(2,1)} %bitcast.27, bf16[256,1152]{1,0:T(8,128)(2,1)} %bitcast.30, bf16[1152,3456]{1,0:T(8,128)(2,1)} %bitcast.21, bf16[8,8]{1,0:T(8,128)(2,1)} %convert_element_type.3.mask_ref), custom_call_target="tpu_custom_call" | custom-call | tf_op jit(solution)/shard_map/temporal/pallas_call | solution.py:225
  226.0 2.5 copy.16
  228.5 26.1 %all_to_all.27 = bf16[2,256,1152]{2,0,1:T(2,128)(2,1)S(1)} all-to-all(bf16[2,256,1152]{2,0,1:T(2,128)(2,1)S(1)} %copy.16), channel_id=1, replica_groups=mesh['y'=4,'zh'=2,'core'=2,'x'=4,'zl'=4] {'y','zh','core'}, dimensions={1} | all-to-all | bytes 2359296 | tf_op jit(solution)/shard_map/all_to_all | solution.py:308
  254.5 1.1 copy.17
  (35 shorter events, 2.4 us)
Async XLA Ops:
  6.5 12.2 %copy-start.6 = (bf16[72,3456]{1,0:T(8,128)(2,1)S(1)}, bf16[72,3456]{1,0:T(8,128)(2,1)}, u32[]{:S(2)}) copy-start(bf16[72,3456]{1,0:T(8,128)(2,1)} %param.18) | copy-start | bytes 1492996
  6.5 59.6 %all-gather.5.cloned.1.call-start = ((), (), s32[]{:S(2)}) async-start(), calls=%async_computation.3 | async-start | bytes 2985984 | tf_op jit(solution)/shard_map/all_gather | solution.py:245
  6.5 10.4 %collective-permute-start.2 = (bf16[72,1152]{1,0:T(8,128)(2,1)}, bf16[72,1152]{1,0:T(8,128)(2,1)S(1)}, u32[]{:S(2)}, u32[]{:S(2)}) collective-permute-start(bf16[72,1152]{1,0:T(8,128)(2,1)} %param.17), channel_id=1, source_target_pairs={{0,35},{1,34},{2,33},{3,32},{32,3},{33,2},{34,1},{35,0},{4,39},{5,... | collective-permute-start | bytes 497672 | tf_op jit(solution)/shard_map/ppermute | solution.py:239
  18.7 139.2 %all-gather.7.cloned.1.call-start = ((), (), s32[]{:S(2)}) async-start(), calls=%async_computation.4 | async-start | bytes 8957952 | tf_op jit(solution)/shard_map/all_gather | solution.py:245
  18.7 15.7 %collective-permute-start.4 = (bf16[72,3456]{1,0:T(8,128)(2,1)S(1)}, bf16[72,3456]{1,0:T(8,128)(2,1)S(1)}, u32[]{:S(2)}, u32[]{:S(2)}) collective-permute-start(bf16[72,3456]{1,0:T(8,128)(2,1)S(1)} %copy-done.6), channel_id=1, source_target_pairs={{0,35},{1,34},{2,33},{3,32},{32,3},{33,2},{34,1},{35,0},{4,39},{5,... | collective-permute-start | bytes 1493000 | tf_op jit(solution)/shard_map/ppermute | solution.py:239
  34.4 1.7 copy-start
  34.5 2.0 copy-start.1
  37.9 40.2 %collective-permute-start = (bf16[2,8,32,1152]{3,2,1,0:T(8,128)(2,1)}, bf16[2,8,32,1152]{3,2,1,0:T(8,128)(2,1)}, u32[]{:S(2)}, u32[]{:S(2)}) collective-permute-start(bf16[2,8,32,1152]{3,2,1,0:T(8,128)(2,1)} %pad_maximum_fusion), channel_id=1, source_target_pairs={{0,1},{1,2},{3,4},{4,5},{5,6},{7,8},{8,9},{9,10},{11,12},{12,13},{... | collective-permute-start | bytes 3538952 | tf_op jit(solution)/shard_map/ppermute | solution.py:272
  40.8 88.3 %collective-permute-start.1 = (bf16[2,8,32,1152]{3,2,1,0:T(8,128)(2,1)}, bf16[2,8,32,1152]{3,2,1,0:T(8,128)(2,1)}, u32[]{:S(2)}, u32[]{:S(2)}) collective-permute-start(bf16[2,8,32,1152]{3,2,1,0:T(8,128)(2,1)} %pad_maximum_fusion), channel_id=1, source_target_pairs={{1,0},{2,1},{4,3},{5,4},{6,5},{8,7},{9,8},{10,9},{12,11},{13,12},{... | collective-permute-start | bytes 3538952 | tf_op jit(solution)/shard_map/ppermute | solution.py:273
  52.9 10.7 %copy-start.7 = (f32[2,1152]{1,0:T(2,128)S(1)}, f32[2,1152]{1,0:T(2,128)}, u32[]{:S(2)}) copy-start(f32[2,1152]{1,0:T(2,128)} %param.19) | copy-start | bytes 27652
  52.9 11.4 %copy-start.11 = (s32[4,6]{1,0:T(4,128)S(1)}, s32[4,6]{1,0:T(4,128)}, u32[]{:S(2)}) copy-start(s32[4,6]{1,0:T(4,128)} %param.15) | copy-start | bytes 292
  52.9 12.0 %copy-start.8 = (f32[1152]{0:T(1024)S(1)}, f32[1152]{0:T(1024)}, u32[]{:S(2)}) copy-start(f32[1152]{0:T(1024)} %param.20) | copy-start | bytes 13828
  52.9 12.6 %copy-start.9 = (f32[1152]{0:T(1024)S(1)}, f32[1152]{0:T(1024)}, u32[]{:S(2)}) copy-start(f32[1152]{0:T(1024)} %param.21) | copy-start | bytes 13828
  54.0 110.8 %collective-permute-start.3 = (bf16[2,8,32,1152]{3,2,1,0:T(8,128)(2,1)}, bf16[2,8,32,1152]{3,2,1,0:T(8,128)(2,1)S(1)}, u32[]{:S(2)}, u32[]{:S(2)}) collective-permute-start(bf16[2,8,32,1152]{3,2,1,0:T(8,128)(2,1)} %pad_maximum_fusion.1), channel_id=1, source_target_pairs={{0,1},{1,2},{3,4},{4,5},{5,6},{7,8},{8,9},{9,10},{11,12},{12,13},{... | collective-permute-start | bytes 3538952 | tf_op jit(solution)/shard_map/ppermute | solution.py:272
  56.0 108.9 %collective-permute-start.5 = (bf16[2,8,32,1152]{3,2,1,0:T(8,128)(2,1)}, bf16[2,8,32,1152]{3,2,1,0:T(8,128)(2,1)S(1)}, u32[]{:S(2)}, u32[]{:S(2)}) collective-permute-start(bf16[2,8,32,1152]{3,2,1,0:T(8,128)(2,1)} %pad_maximum_fusion.1), channel_id=1, source_target_pairs={{1,0},{2,1},{4,3},{5,4},{6,5},{8,7},{9,8},{10,9},{12,11},{13,12},{... | collective-permute-start | bytes 3538952 | tf_op jit(solution)/shard_map/ppermute | solution.py:273
  149.0 37.1 %all-to-all-start = ((bf16[16,16,1152]{2,1,0:T(8,128)(2,1)}), bf16[16,16,1152]{2,1,0:T(8,128)(2,1)S(1)}, u32[]{:S(2)}, u32[]{:S(2)}) async-start(bf16[16,16,1152]{2,1,0:T(8,128)(2,1)} %bitcast.28), calls=%async_computation | async-start | bytes 1179648 | tf_op jit(solution)/shard_map/all_to_all | solution.py:304
  164.8 1.0 copy-start.4
  164.8 1.4 copy-start.5
  186.1 9.7 %copy-start.10 = (s32[8,8]{1,0:T(8,128)S(1)}, s32[8,8]{1,0:T(8,128)}, u32[]{:S(2)}) copy-start(s32[8,8]{1,0:T(8,128)} %param.16) | copy-start | bytes 772
  186.1 25.1 %copy-start.2 = (bf16[16,16,1152]{2,1,0:T(8,128)(2,1)}, bf16[16,16,1152]{2,1,0:T(8,128)(2,1)S(1)}, u32[]{:S(2)}) copy-start(bf16[16,16,1152]{2,1,0:T(8,128)(2,1)S(1)} %all-to-all-done) | copy-start | bytes 1769476
  186.1 25.1 %all-to-all-start.1 = ((bf16[16,16,1152]{2,1,0:T(8,128)(2,1)}), bf16[16,16,1152]{2,1,0:T(8,128)(2,1)S(1)}, u32[]{:S(2)}, u32[]{:S(2)}) async-start(bf16[16,16,1152]{2,1,0:T(8,128)(2,1)} %bitcast.29), calls=%async_computation.1 | async-start | bytes 1179648 | tf_op jit(solution)/shard_map/all_to_all | solution.py:304
  211.2 0.8 copy-start.3
Sparse Core Ops, SparseCore 0:
  18.8 31.5 all-gather.4
  52.2 50.9 all-gather.6
where the time goes:
time: 267 us; the launch traced here: 263 us
  waiting for transfers between devices  89.3 us (33%)
  starting transfers between devices  53.7 us (20%)
  Pallas kernels  53.7 us (20%)
  blocking collectives  26.1 us (10%)
  local copies, waits for them, and re-layouts  20.4 us (8%)
  between operations  13.6 us (5%)
  other arithmetic  5.7 us (2%)
    ppermute x2, waiting for transfers between devices, local(): high = lax.ppermute(both, ROW_AXIS, up)  51.1 us
    pallas_call x2, Pallas kernels, spatial(): pl.pallas_call(spatial_kernel, out_shape=jax.ShapeDtypeStruct((height, br...  39.7 us
    all_to_all x1, blocking collectives, local(): lax.all_to_all(done, FRAME_AXIS, split_axis=1, concat_axis=1, tiled=True)  26.1 us
    ppermute x2, starting transfers between devices, local(): high = lax.ppermute(both, ROW_AXIS, up)  19.7 us
    all_to_all x2, starting transfers between devices, local(): lax.all_to_all(normed, FRAME_AXIS, split_axis=0, concat_axis=0, tiled=True)  18.5 us
    ppermute x2, waiting for transfers between devices, mirrored(): return lax.ppermute(weight, ('zh', 'zl'), [(i, 7 - i) for i in range(8)])  15.4 us
    all_to_all x2, waiting for transfers between devices, local(): lax.all_to_all(normed, FRAME_AXIS, split_axis=0, concat_axis=0, tiled=True)  14.8 us
    pallas_call x1, Pallas kernels, temporal(): pl.pallas_call(temporal_kernel, out_shape=jax.ShapeDtypeStruct((2, per_fr...  14 us
  transfers between devices with their start and end apart: 10, of which 5 were waited for; matrix products, arithmetic and copies ran while one was open for 7% of the time, Pallas kernels for 15%

commit v1 on v0

--- a/solution.py
+++ b/solution.py
@@ -21,6 +21,7 @@
 PAIRS = HEADS // 2
 WINDOW = 256
 LANES = 128
+CHUNK = 64
 NT = (((1,), (1,)), ((), ()))
 RATE = (1.0 / math.sqrt(HEAD)) * math.log2(math.e)
 
@@ -32,32 +33,44 @@
     return first, second
 
 
-def soft(scores):
-    peak = jnp.max(scores, axis=-1, keepdims=True)
-    powers = jnp.exp2((scores - peak) * RATE)
-    total = jnp.sum(powers, axis=-1, keepdims=True)
-    return (powers * (1.0 / total)).astype(jnp.bfloat16)
-
-
-def attend(window_of, bias):
+def attend(window_of, bias, scored, weighed):
+    rows = scored.shape[1] // 2
+
+    def score(pair):
+        first, second = pair_masks(pair)
+        queries, keys, _ = window_of(pair)
+        zero = jnp.zeros_like(queries)
+        for side, mask in enumerate((first, second)):
+            scored[pair % 2, side * rows : (side + 1) * rows, :] = lax.dot_general(
+                jnp.where(mask, queries, zero), keys, NT, preferred_element_type=jnp.float32
+            )
+
+    def soften(pair):
+        for at in range(0, 2 * rows, CHUNK):
+            scores = scored[pair % 2, at : at + CHUNK, :]
+            if bias is not None:
+                scores = scores + bias[at % rows : at % rows + CHUNK, :]
+            peak = jnp.max(scores, axis=-1, keepdims=True)
+            powers = jnp.exp2((scores - peak) * RATE)
+            total = jnp.sum(powers, axis=-1, keepdims=True)
+            weighed[pair % 2, at : at + CHUNK, :] = (powers * (1.0 / total)).astype(jnp.bfloat16)
+
     carried = None
-    for pair in range(PAIRS):
-        first, second = pair_masks(pair)
-        queries, keys, values = window_of(pair)
-        rows = queries.shape[0]
-        zero = jnp.zeros_like(queries)
-        both = jnp.concatenate(
-            [jnp.where(first, queries, zero), jnp.where(second, queries, zero)], axis=0
-        )
-        scores = lax.dot_general(both, keys, NT, preferred_element_type=jnp.float32)
-        if bias is not None:
-            scores = scores + jnp.concatenate([bias, bias], axis=0)
-        weights = soft(scores)
-        out = jnp.dot(weights, values, preferred_element_type=jnp.float32)
-        out = jnp.where(first, out[:rows], jnp.where(second, out[rows:], 0.0))
-        low, high = out[:, :LANES], out[:, LANES:]
-        yield pair, low if carried is None else low + carried
-        carried = high
+    score(0)
+    for pair in range(PAIRS + 1):
+        if pair + 1 < PAIRS:
+            score(pair + 1)
+        if pair > 0:
+            done = pair - 1
+            first, second = pair_masks(done)
+            values = window_of(done)[2]
+            out = jnp.dot(weighed[done % 2], values, preferred_element_type=jnp.float32)
+            out = jnp.where(first, out[:rows], jnp.where(second, out[rows:], 0.0))
+            low, high = out[:, :LANES], out[:, LANES:]
+            yield done, low if carried is None else low + carried
+            carried = high
+        if pair < PAIRS:
+            soften(pair)
     yield PAIRS, carried
 
 
@@ -81,6 +94,8 @@
     vw,
     heads,
     acc,
+    scored,
+    weighed,
 ):
     size = TILE * TILE
 
@@ -112,7 +127,7 @@
             lanes = slice(LANES * pair, LANES * pair + WINDOW)
             return qt[w, :, lanes], kw[:, lanes], vw[:, lanes]
 
-        for block, value in attend(window_of, None):
+        for block, value in attend(window_of, None, scored, weighed):
             heads[pl.ds(pl.multiple_of(w * size, size), size), block * LANES : (block + 1) * LANES] = (
                 value.astype(jnp.bfloat16)
             )
@@ -176,6 +191,8 @@
                 pltpu.VMEM((384, D), bf16),
                 pltpu.VMEM((tokens, D), bf16),
                 pltpu.VMEM((tokens, D), jnp.float32),
+                pltpu.VMEM((2, 128, 384), jnp.float32),
+                pltpu.VMEM((2, 128, 384), bf16),
             ],
         ),
         compiler_params=pltpu.CompilerParams(vmem_limit_bytes=56 << 20),
@@ -183,7 +200,7 @@
     )(ids, q, k, v, low, high, residual, weight, pos, shift, scale)
 
 
-def temporal_kernel(even_ref, odd_ref, w_ref, mask_ref, out_ref, xs, proj, done):
+def temporal_kernel(even_ref, odd_ref, w_ref, mask_ref, out_ref, xs, proj, done, bias, scored, weighed):
     per_frame = even_ref.shape[0]
     spots = done.shape[1]
     peers = per_frame // spots
@@ -196,7 +213,7 @@
     spread = (near == lax.broadcasted_iota(jnp.int32, (rows, blocks), 1)).astype(jnp.bfloat16)
     reach = jnp.dot(spread, mask_ref[...], preferred_element_type=jnp.float32).astype(jnp.bfloat16)
     allowed = lax.dot_general(reach, spread, NT, preferred_element_type=jnp.float32)
-    bias = jnp.where((allowed > 0.5) & (r % TILE == c % TILE), 0.0, -1e30)
+    bias[...] = jnp.where((allowed > 0.5) & (r % TILE == c % TILE), 0.0, -1e30)
     for f, src in enumerate((even_ref, odd_ref)):
         whole = src[...].astype(jnp.float32).reshape(peers, spots, D)
         for g in range(spots // TILE):
@@ -210,12 +227,12 @@
             here = slice(g * rows, (g + 1) * rows)
             return tuple(proj[here, base + lane : base + lane + WINDOW] for base in (0, D, 2 * D))
 
-        for block, value in attend(window_of, bias):
+        for block, value in attend(window_of, bias, scored, weighed):
             done[:, g * TILE : (g + 1) * TILE, block * LANES : (block + 1) * LANES] = value.reshape(
                 2 * peers, TILE, LANES
             )
     for f in range(2):
-        out_ref[f] = done[f * peers : (f + 1) * peers].reshape(per_frame, D).astype(jnp.bfloat16)
+        out_ref[:, f] = done[f * peers : (f + 1) * peers].astype(jnp.bfloat16)
 
 
 def temporal(even, odd, weight, mask):
@@ -224,11 +241,14 @@
     spots = per_frame // peers
     return pl.pallas_call(
         temporal_kernel,
-        out_shape=jax.ShapeDtypeStruct((2, per_frame, D), jnp.bfloat16),
+        out_shape=jax.ShapeDtypeStruct((peers, 2, spots, D), jnp.bfloat16),
         scratch_shapes=[
             pltpu.VMEM((2 * per_frame, D), jnp.bfloat16),
             pltpu.VMEM((2 * per_frame, 3 * D), jnp.bfloat16),
             pltpu.VMEM((2 * peers, spots, D), jnp.float32),
+            pltpu.VMEM((256, 256), jnp.float32),
+            pltpu.VMEM((2, 512, 256), jnp.float32),
+            pltpu.VMEM((2, 512, 256), jnp.bfloat16),
         ],
         compiler_params=pltpu.CompilerParams(vmem_limit_bytes=56 << 20),
         name="temporal",
@@ -305,8 +325,8 @@
         )
     mask = block_mask.astype(jnp.bfloat16)
     done = temporal(arrived[0], arrived[1], w_qkv, mask)
-    returned = lax.all_to_all(done, FRAME_AXIS, split_axis=1, concat_axis=1, tiled=True)
-    return returned.reshape(frames_here, height, breadth, channels)
+    returned = lax.all_to_all(done, FRAME_AXIS, split_axis=0, concat_axis=0, tiled=True)
+    return jnp.transpose(returned, (1, 0, 2, 3)).reshape(frames_here, height, breadth, channels)
 
 
 def solution(mesh):

time: 267 us -> 259 us (0.970)
  the two profiles are of different devices: /device:TPU:38 before, /device:TPU:33 now
where the time goes in v1:
time: 259 us
  waiting for transfers between devices  87.9 us (34%)
  starting transfers between devices  58.1 us (22%)
  Pallas kernels  40.4 us (16%)
  blocking collectives  35.2 us (14%)
  local copies, waits for them, and re-layouts  17.9 us (7%)
  between operations  13.6 us (5%)
  other arithmetic  5.7 us (2%)
    ppermute x2, waiting for transfers between devices, local(): high = lax.ppermute(both, ROW_AXIS, up)  51.6 us
    all_to_all x1, blocking collectives, local(): lax.all_to_all(done, FRAME_AXIS, split_axis=0, concat_axis=0, tiled=True)  35.2 us
    pallas_call x2, Pallas kernels, spatial(): pl.pallas_call(spatial_kernel, out_shape=jax.ShapeDtypeStruct((height, br...  27.3 us
    ppermute x2, starting transfers between devices, local(): high = lax.ppermute(both, ROW_AXIS, up)  22.3 us
    all_to_all x2, starting transfers between devices, local(): lax.all_to_all(normed, FRAME_AXIS, split_axis=0, concat_axis=0, tiled=True)  21.6 us
    all_to_all x2, waiting for transfers between devices, local(): lax.all_to_all(normed, FRAME_AXIS, split_axis=0, concat_axis=0, tiled=True)  15.2 us
    ppermute x2, waiting for transfers between devices, mirrored(): return lax.ppermute(weight, ('zh', 'zl'), [(i, 7 - i) for i in range(8)])  14.6 us
    pallas_call x1, Pallas kernels, temporal(): pl.pallas_call(temporal_kernel, out_shape=jax.ShapeDtypeStruct((peers, 2,...  13.1 us
  transfers between devices with their start and end apart: 10, of which 6 were waited for; matrix products, arithmetic and copies ran while one was open for 7% of the time, Pallas kernels for 11%

profile of v1, /device:TPU:33, one launch (start us, length us, event | category | flops | bytes accessed | tf_op | source)
XLA Modules:
  0.0 258.7 jit_solution(13395634630244915007)
XLA Ops:
  6.5 5.6 %collective-permute-start.2 = (bf16[72,1152]{1,0:T(8,128)(2,1)}, bf16[72,1152]{1,0:T(8,128)(2,1)S(1)}, u32[]{:S(2)}, u32[]{:S(2)}) collective-permute-start(bf16[72,1152]{1,0:T(8,128)(2,1)} %param.17), channel_id=1, source_target_pairs={{0,35},{1,34},{2,33},{3,32},{32,3},{33,2},{34,1},{35,0},{4,39},{5,... | collective-permute-start | bytes 497672 | tf_op jit(solution)/shard_map/ppermute | solution.py:259
  12.1 4.2 %collective-permute-done.2 = bf16[72,1152]{1,0:T(8,128)(2,1)S(1)} collective-permute-done((bf16[72,1152]{1,0:T(8,128)(2,1)}, bf16[72,1152]{1,0:T(8,128)(2,1)S(1)}, u32[]{:S(2)}, u32[]{:S(2)}) %collective-permute-start.2) | collective-permute-done | bytes 165920 | tf_op jit(solution)/shard_map/ppermute | solution.py:259
  16.3 0.9 select_bitcast_fusion.3
  17.3 0.7 pad_maximum_fusion.3
  18.1 4.3 %collective-permute-start.4 = (bf16[72,3456]{1,0:T(8,128)(2,1)S(1)}, bf16[72,3456]{1,0:T(8,128)(2,1)S(1)}, u32[]{:S(2)}, u32[]{:S(2)}) collective-permute-start(bf16[72,3456]{1,0:T(8,128)(2,1)S(1)} %copy-done.6), channel_id=1, source_target_pairs={{0,35},{1,34},{2,33},{3,32},{32,3},{33,2},{34,1},{35,0},{4,39},{5,... | collective-permute-start | bytes 1493000 | tf_op jit(solution)/shard_map/ppermute | solution.py:259
  22.4 10.4 %collective-permute-done.4 = bf16[72,3456]{1,0:T(8,128)(2,1)S(1)} collective-permute-done((bf16[72,3456]{1,0:T(8,128)(2,1)S(1)}, bf16[72,3456]{1,0:T(8,128)(2,1)S(1)}, u32[]{:S(2)}, u32[]{:S(2)}) %collective-permute-start.4) | collective-permute-done | bytes 497696 | tf_op jit(solution)/shard_map/ppermute | solution.py:259
  32.9 1.1 pad_maximum_fusion.2
  35.2 1.1 pad_maximum_fusion
  36.4 2.4 collective-permute-start
  38.8 14.1 %collective-permute-start.1 = (bf16[2,8,32,1152]{3,2,1,0:T(8,128)(2,1)}, bf16[2,8,32,1152]{3,2,1,0:T(8,128)(2,1)}, u32[]{:S(2)}, u32[]{:S(2)}) collective-permute-start(bf16[2,8,32,1152]{3,2,1,0:T(8,128)(2,1)} %pad_maximum_fusion), channel_id=1, source_target_pairs={{1,0},{2,1},{4,3},{5,4},{6,5},{8,7},{9,8},{10,9},{12,11},{13,12},{... | collective-permute-start | bytes 3538952 | tf_op jit(solution)/shard_map/ppermute | solution.py:293
  52.9 1.1 pad_maximum_fusion.1
  54.0 1.9 collective-permute-start.3
  55.9 8.3 %collective-permute-start.5 = (bf16[2,8,32,1152]{3,2,1,0:T(8,128)(2,1)}, bf16[2,8,32,1152]{3,2,1,0:T(8,128)(2,1)S(1)}, u32[]{:S(2)}, u32[]{:S(2)}) collective-permute-start(bf16[2,8,32,1152]{3,2,1,0:T(8,128)(2,1)} %pad_maximum_fusion.1), channel_id=1, source_target_pairs={{1,0},{2,1},{4,3},{5,4},{6,5},{8,7},{9,8},{10,9},{12,11},{13,12},{... | collective-permute-start | bytes 3538952 | tf_op jit(solution)/shard_map/ppermute | solution.py:293
  64.2 0.6 fusion.8
  64.9 0.7 reshape.32.ids
  65.5 0.6 reshape.35.shift_ref
  66.1 0.6 reshape.36.scale_ref
  66.7 4.0 %copy.17 = bf16[4,2,2,72,1152]{4,3,1,2,0:T(8,128)(2,1)} copy(bf16[4,2,2,72,1152]{4,3,2,1,0:T(8,128)(2,1)} %bitcast.27) | data formatting | bytes 5308416 | tf_op jit(solution)/shard_map/reshape | solution.py:267
  70.8 6.4 %collective-permute-done.low = bf16[2,8,32,1152]{3,2,1,0:T(8,128)(2,1)} collective-permute-done((bf16[2,8,32,1152]{3,2,1,0:T(8,128)(2,1)}, bf16[2,8,32,1152]{3,2,1,0:T(8,128)(2,1)}, u32[]{:S(2)}, u32[]{:S(2)}) %collective-permute-start) | collective-permute-done | bytes 1179680 | tf_op jit(solution)/shard_map/ppermute | solution.py:292
  77.1 51.5 %collective-permute-done.1.high = bf16[2,8,32,1152]{3,2,1,0:T(8,128)(2,1)} collective-permute-done((bf16[2,8,32,1152]{3,2,1,0:T(8,128)(2,1)}, bf16[2,8,32,1152]{3,2,1,0:T(8,128)(2,1)}, u32[]{:S(2)}, u32[]{:S(2)}) %collective-permute-start.1) | collective-permute-done | bytes 1179680 | tf_op jit(solution)/shard_map/ppermute | solution.py:293
  128.6 13.7 %spatial.2 = bf16[8,32,1152]{2,1,0:T(8,128)(2,1)} custom-call(s32[24]{0:T(128)} %reshape.32.ids, bf16[2,8,32,1152]{3,2,1,0:T(8,128)(2,1)} %q_ref.3, bf16[2,8,32,1152]{3,2,1,0:T(8,128)(2,1)} %k_own.3, bf16[2,8,32,1152]{3,2,1,0:T(8,128)(2,1)} %v_own.3, bf16[2,8,32,1152]{3,2,1,0:T(8,128)(2,1)} %collective-permute-done.low, ...), custom_call_target="tpu_custom_call" | custom-call | tf_op jit(solution)/shard_map/spatial/pallas_call | solution.py:167
  142.3 10.9 %all-to-all-start = ((bf16[16,16,1152]{2,1,0:T(8,128)(2,1)}), bf16[16,16,1152]{2,1,0:T(8,128)(2,1)S(1)}, u32[]{:S(2)}, u32[]{:S(2)}) async-start(bf16[16,16,1152]{2,1,0:T(8,128)(2,1)} %bitcast.29), calls=%async_computation | async-start | bytes 1179648 | tf_op jit(solution)/shard_map/all_to_all | solution.py:324
  153.2 6.9 %copy.18 = bf16[4,2,2,72,3456]{4,3,1,2,0:T(8,128)(2,1)} copy(bf16[4,2,2,72,3456]{4,3,2,1,0:T(8,128)(2,1)} %bitcast.25) | data formatting | bytes 15925248 | tf_op jit(solution)/shard_map/reshape | solution.py:267
  160.2 0.9 copy-done.4
  161.5 13.7 %spatial.3 = bf16[8,32,1152]{2,1,0:T(8,128)(2,1)} custom-call(s32[24]{0:T(128)} %reshape.32.ids, bf16[2,8,32,1152]{3,2,1,0:T(8,128)(2,1)} %q_ref.3, bf16[2,8,32,1152]{3,2,1,0:T(8,128)(2,1)} %k_own.3, bf16[2,8,32,1152]{3,2,1,0:T(8,128)(2,1)} %v_own.3, bf16[2,8,32,1152]{3,2,1,0:T(8,128)(2,1)} %copy-done.4, bf16[2,8,32,1152]{3,2,1,0:T(8,128)(2,1)} %copy-done.5, ...), custom_call_target="tpu_custom_call" | custom-call | tf_op jit(solution)/shard_map/spatial/pallas_call | solution.py:167
  175.2 10.6 %all-to-all-start.1 = ((bf16[16,16,1152]{2,1,0:T(8,128)(2,1)}), bf16[16,16,1152]{2,1,0:T(8,128)(2,1)S(1)}, u32[]{:S(2)}, u32[]{:S(2)}) async-start(bf16[16,16,1152]{2,1,0:T(8,128)(2,1)} %bitcast.30), calls=%async_computation.1 | async-start | bytes 1179648 | tf_op jit(solution)/shard_map/all_to_all | solution.py:324
  185.8 0.6 convert_element_type.3.mask_ref
  186.4 15.2 %all-to-all-done.1 = bf16[16,16,1152]{2,1,0:T(8,128)(2,1)S(1)} async-done(((bf16[16,16,1152]{2,1,0:T(8,128)(2,1)}), bf16[16,16,1152]{2,1,0:T(8,128)(2,1)S(1)}, u32[]{:S(2)}, u32[]{:S(2)}) %all-to-all-start.1) | async-done | bytes 589856 | tf_op jit(solution)/shard_map/all_to_all | solution.py:324
  201.7 0.8 copy-done.3
  202.5 13.1 %temporal.1 = bf16[16,2,16,1152]{3,2,1,0:T(8,128)(2,1)} custom-call(bf16[256,1152]{1,0:T(8,128)(2,1)} %bitcast.28, bf16[256,1152]{1,0:T(8,128)(2,1)} %bitcast.31, bf16[1152,3456]{1,0:T(8,128)(2,1)} %bitcast.22, bf16[8,8]{1,0:T(8,128)(2,1)} %convert_element_type.3.mask_ref), custom_call_target="tpu_custom_call" | custom-call | tf_op jit(solution)/shard_map/temporal/pallas_call | solution.py:242
  215.6 35.2 %all_to_all.27 = bf16[16,2,16,1152]{3,2,1,0:T(8,128)(2,1)S(1)} all-to-all(bf16[16,2,16,1152]{3,2,1,0:T(8,128)(2,1)} %temporal.1), channel_id=1, replica_groups=mesh['y'=4,'zh'=2,'core'=2,'x'=4,'zl'=4] {'y','zh','core'}, dimensions={0} | all-to-all | bytes 2359296 | tf_op jit(solution)/shard_map/all_to_all | solution.py:328
  250.7 1.1 copy.19
  (34 shorter events, 1.9 us)
Async XLA Ops:
  6.5 11.5 %copy-start.6 = (bf16[72,3456]{1,0:T(8,128)(2,1)S(1)}, bf16[72,3456]{1,0:T(8,128)(2,1)}, u32[]{:S(2)}) copy-start(bf16[72,3456]{1,0:T(8,128)(2,1)} %param.18) | copy-start | bytes 1492996
  6.5 60.2 %all-gather.5.cloned.1.call-start = ((), (), s32[]{:S(2)}) async-start(), calls=%async_computation.3 | async-start | bytes 2985984 | tf_op jit(solution)/shard_map/all_gather | solution.py:265
  6.5 9.8 %collective-permute-start.2 = (bf16[72,1152]{1,0:T(8,128)(2,1)}, bf16[72,1152]{1,0:T(8,128)(2,1)S(1)}, u32[]{:S(2)}, u32[]{:S(2)}) collective-permute-start(bf16[72,1152]{1,0:T(8,128)(2,1)} %param.17), channel_id=1, source_target_pairs={{0,35},{1,34},{2,33},{3,32},{32,3},{33,2},{34,1},{35,0},{4,39},{5,... | collective-permute-start | bytes 497672 | tf_op jit(solution)/shard_map/ppermute | solution.py:259
  18.0 135.2 %all-gather.7.cloned.1.call-start = ((), (), s32[]{:S(2)}) async-start(), calls=%async_computation.4 | async-start | bytes 8957952 | tf_op jit(solution)/shard_map/all_gather | solution.py:265
  18.1 14.7 %collective-permute-start.4 = (bf16[72,3456]{1,0:T(8,128)(2,1)S(1)}, bf16[72,3456]{1,0:T(8,128)(2,1)S(1)}, u32[]{:S(2)}, u32[]{:S(2)}) collective-permute-start(bf16[72,3456]{1,0:T(8,128)(2,1)S(1)} %copy-done.6), channel_id=1, source_target_pairs={{0,35},{1,34},{2,33},{3,32},{32,3},{33,2},{34,1},{35,0},{4,39},{5,... | collective-permute-start | bytes 1493000 | tf_op jit(solution)/shard_map/ppermute | solution.py:259
  32.9 1.7 copy-start
  32.9 2.1 copy-start.1
  36.4 40.8 %collective-permute-start = (bf16[2,8,32,1152]{3,2,1,0:T(8,128)(2,1)}, bf16[2,8,32,1152]{3,2,1,0:T(8,128)(2,1)}, u32[]{:S(2)}, u32[]{:S(2)}) collective-permute-start(bf16[2,8,32,1152]{3,2,1,0:T(8,128)(2,1)} %pad_maximum_fusion), channel_id=1, source_target_pairs={{0,1},{1,2},{3,4},{4,5},{5,6},{7,8},{8,9},{9,10},{11,12},{12,13},{... | collective-permute-start | bytes 3538952 | tf_op jit(solution)/shard_map/ppermute | solution.py:292
  38.8 89.8 %collective-permute-start.1 = (bf16[2,8,32,1152]{3,2,1,0:T(8,128)(2,1)}, bf16[2,8,32,1152]{3,2,1,0:T(8,128)(2,1)}, u32[]{:S(2)}, u32[]{:S(2)}) collective-permute-start(bf16[2,8,32,1152]{3,2,1,0:T(8,128)(2,1)} %pad_maximum_fusion), channel_id=1, source_target_pairs={{1,0},{2,1},{4,3},{5,4},{6,5},{8,7},{9,8},{10,9},{12,11},{13,12},{... | collective-permute-start | bytes 3538952 | tf_op jit(solution)/shard_map/ppermute | solution.py:293
  52.8 11.4 %copy-start.7 = (f32[2,1152]{1,0:T(2,128)S(1)}, f32[2,1152]{1,0:T(2,128)}, u32[]{:S(2)}) copy-start(f32[2,1152]{1,0:T(2,128)} %param.19) | copy-start | bytes 27652
  52.8 12.0 %copy-start.11 = (s32[4,6]{1,0:T(4,128)S(1)}, s32[4,6]{1,0:T(4,128)}, u32[]{:S(2)}) copy-start(s32[4,6]{1,0:T(4,128)} %param.15) | copy-start | bytes 292
  52.9 12.7 %copy-start.8 = (f32[1152]{0:T(1024)S(1)}, f32[1152]{0:T(1024)}, u32[]{:S(2)}) copy-start(f32[1152]{0:T(1024)} %param.20) | copy-start | bytes 13828
  52.9 13.3 %copy-start.9 = (f32[1152]{0:T(1024)S(1)}, f32[1152]{0:T(1024)}, u32[]{:S(2)}) copy-start(f32[1152]{0:T(1024)} %param.21) | copy-start | bytes 13828
  54.0 106.1 %collective-permute-start.3 = (bf16[2,8,32,1152]{3,2,1,0:T(8,128)(2,1)}, bf16[2,8,32,1152]{3,2,1,0:T(8,128)(2,1)S(1)}, u32[]{:S(2)}, u32[]{:S(2)}) collective-permute-start(bf16[2,8,32,1152]{3,2,1,0:T(8,128)(2,1)} %pad_maximum_fusion.1), channel_id=1, source_target_pairs={{0,1},{1,2},{3,4},{4,5},{5,6},{7,8},{8,9},{9,10},{11,12},{12,13},{... | collective-permute-start | bytes 3538952 | tf_op jit(solution)/shard_map/ppermute | solution.py:292
  55.9 104.3 %collective-permute-start.5 = (bf16[2,8,32,1152]{3,2,1,0:T(8,128)(2,1)}, bf16[2,8,32,1152]{3,2,1,0:T(8,128)(2,1)S(1)}, u32[]{:S(2)}, u32[]{:S(2)}) collective-permute-start(bf16[2,8,32,1152]{3,2,1,0:T(8,128)(2,1)} %pad_maximum_fusion.1), channel_id=1, source_target_pairs={{1,0},{2,1},{4,3},{5,4},{6,5},{8,7},{9,8},{10,9},{12,11},{13,12},{... | collective-permute-start | bytes 3538952 | tf_op jit(solution)/shard_map/ppermute | solution.py:293
  142.3 32.9 %all-to-all-start = ((bf16[16,16,1152]{2,1,0:T(8,128)(2,1)}), bf16[16,16,1152]{2,1,0:T(8,128)(2,1)S(1)}, u32[]{:S(2)}, u32[]{:S(2)}) async-start(bf16[16,16,1152]{2,1,0:T(8,128)(2,1)} %bitcast.29), calls=%async_computation | async-start | bytes 1179648 | tf_op jit(solution)/shard_map/all_to_all | solution.py:324
  160.1 1.0 copy-start.4
  160.2 1.3 copy-start.5
  175.2 10.7 %copy-start.10 = (s32[8,8]{1,0:T(8,128)S(1)}, s32[8,8]{1,0:T(8,128)}, u32[]{:S(2)}) copy-start(s32[8,8]{1,0:T(8,128)} %param.16) | copy-start | bytes 772
  175.2 26.5 %copy-start.2 = (bf16[16,16,1152]{2,1,0:T(8,128)(2,1)}, bf16[16,16,1152]{2,1,0:T(8,128)(2,1)S(1)}, u32[]{:S(2)}) copy-start(bf16[16,16,1152]{2,1,0:T(8,128)(2,1)S(1)} %all-to-all-done) | copy-start | bytes 1769476
  175.2 26.5 %all-to-all-start.1 = ((bf16[16,16,1152]{2,1,0:T(8,128)(2,1)}), bf16[16,16,1152]{2,1,0:T(8,128)(2,1)S(1)}, u32[]{:S(2)}, u32[]{:S(2)}) async-start(bf16[16,16,1152]{2,1,0:T(8,128)(2,1)} %bitcast.30), calls=%async_computation.1 | async-start | bytes 1179648 | tf_op jit(solution)/shard_map/all_to_all | solution.py:324
  201.7 0.8 copy-start.3
Sparse Core Ops, SparseCore 0:
  18.1 32.6 all-gather.4
  52.7 50.9 all-gather.6

commit v2 on v1

--- a/solution.py
+++ b/solution.py
@@ -96,8 +96,12 @@
     acc,
     scored,
     weighed,
+    w_buf,
+    sem,
 ):
     size = TILE * TILE
+    fetch = pltpu.make_async_copy(w_ref, w_buf, sem)
+    fetch.start()
 
     def tile_up(i, _):
         for dst, base, src in (
@@ -134,7 +138,8 @@
         return 0
 
     lax.fori_loop(0, TILES_WIDE, column, 0)
-    acc[...] = jnp.dot(heads[...], w_ref[...], preferred_element_type=jnp.float32)
+    fetch.wait()
+    acc[...] = jnp.dot(heads[...], w_buf[...], preferred_element_type=jnp.float32)
 
     def finish(i, _):
         added = jnp.concatenate(
@@ -177,7 +182,7 @@
                 halo,
                 halo,
                 own,
-                pl.BlockSpec((D, D), lambda g, s: (0, 0)),
+                pl.BlockSpec(memory_space=pl.ANY),
                 row,
                 row,
                 row,
@@ -193,6 +198,8 @@
                 pltpu.VMEM((tokens, D), jnp.float32),
                 pltpu.VMEM((2, 128, 384), jnp.float32),
                 pltpu.VMEM((2, 128, 384), bf16),
+                pltpu.VMEM((D, D), bf16),
+                pltpu.SemaphoreType.DMA(()),
             ],
         ),
         compiler_params=pltpu.CompilerParams(vmem_limit_bytes=56 << 20),
@@ -200,7 +207,10 @@
     )(ids, q, k, v, low, high, residual, weight, pos, shift, scale)
 
 
-def temporal_kernel(even_ref, odd_ref, w_ref, mask_ref, out_ref, xs, proj, done, bias, scored, weighed):
+def temporal_kernel(even_ref, odd_ref, w_ref, mask_ref, out_ref, xs, proj, done, bias, scored, weighed, w_buf, sems):
+    fetches = [pltpu.make_async_copy(w_ref.at[i], w_buf.at[i], sems.at[i]) for i in range(3)]
+    for fetch in fetches:
+        fetch.start()
     per_frame = even_ref.shape[0]
     spots = done.shape[1]
     peers = per_frame // spots
@@ -219,7 +229,11 @@
         for g in range(spots // TILE):
             part = whole[:, g * TILE : (g + 1) * TILE, :].reshape(half, D)
             xs[g * rows + f * half : g * rows + (f + 1) * half, :] = part.astype(jnp.bfloat16)
-    proj[...] = jnp.dot(xs[...], w_ref[...], preferred_element_type=jnp.float32).astype(jnp.bfloat16)
+    for i, fetch in enumerate(fetches):
+        fetch.wait()
+        proj[:, i * D : (i + 1) * D] = jnp.dot(
+            xs[...], w_buf[i], preferred_element_type=jnp.float32
+        ).astype(jnp.bfloat16)
     for g in range(spots // TILE):
 
         def window_of(pair):
@@ -249,23 +263,32 @@
             pltpu.VMEM((256, 256), jnp.float32),
             pltpu.VMEM((2, 512, 256), jnp.float32),
             pltpu.VMEM((2, 512, 256), jnp.bfloat16),
+            pltpu.VMEM((3, D, D), jnp.bfloat16),
+            pltpu.SemaphoreType.DMA((3,)),
+        ],
+        in_specs=[
+            pl.BlockSpec(memory_space=pltpu.VMEM),
+            pl.BlockSpec(memory_space=pltpu.VMEM),
+            pl.BlockSpec(memory_space=pl.ANY),
+            pl.BlockSpec(memory_space=pltpu.VMEM),
         ],
         compiler_params=pltpu.CompilerParams(vmem_limit_bytes=56 << 20),
         name="temporal",
     )(even, odd, weight, mask)
 
 
-def mirrored(weight):
-    return lax.ppermute(weight, ("zh", "zl"), [(i, 7 - i) for i in range(8)])
-
-
-def gathered(weight, other):
+def gathered(out_weight, qkv_weight):
+    rows, channels = out_weight.shape
+    at = lax.axis_index("x") * channels
+    every = jnp.concatenate((out_weight, qkv_weight), axis=1)
+    mine = lax.dynamic_slice_in_dim(every, at, channels, axis=1)
+    other = lax.ppermute(mine, ("zh", "zl"), [(i, 7 - i) for i in range(8)])
     first = lax.axis_index("zh") == 0
-    pair = jnp.stack((jnp.where(first, weight, other), jnp.where(first, other, weight)), 0)
-    full = lax.all_gather(pair, ("y", "core"), axis=0, tiled=False)
-    rows, cols = weight.shape
-    full = full.reshape(4, 2, 2, rows, cols)
-    return jnp.transpose(full, (0, 2, 1, 3, 4)).reshape(16 * rows, cols)
+    pair = jnp.stack((jnp.where(first, mine, other), jnp.where(first, other, mine)), 0)
+    full = lax.all_gather(pair, ("x", "y", "core"), axis=0, tiled=False)
+    full = full.reshape(4, 4, 2, 2, rows, channels)
+    grouped = [jnp.transpose(part, (0, 1, 3, 2, 4, 5)) for part in (full[:1], full[1:])]
+    return grouped[0].reshape(channels, channels), grouped[1].reshape(3, channels, channels)
 
 
 def local(
@@ -292,8 +315,7 @@
         low = lax.ppermute(both, ROW_AXIS, down)
         high = lax.ppermute(both, ROW_AXIS, up)
         moved.append((low, high))
-    w_out = gathered(out_weight, mirrored(out_weight))
-    w_qkv = gathered(qkv_weight, mirrored(qkv_weight))
+    w_out, w_qkv = gathered(out_weight, qkv_weight)
     tile_row_here = (lax.axis_index(ROW_AXIS) + 1) % 4
     ids = (
         (neighbour_list // TILES_WIDE - tile_row_here + 1) * TILES_WIDE

time: 259 us -> 266 us (1.027)
  the two profiles are of different devices: /device:TPU:33 before, /device:TPU:96 now
where the time goes in v2:
time: 266 us; the launch traced here: 265 us
  waiting for transfers between devices  131 us (49%)
  Pallas kernels  38.9 us (15%)
  starting transfers between devices  36.5 us (14%)
  blocking collectives  25.5 us (10%)
  local copies, waits for them, and re-layouts  15.3 us (6%)
  between operations  13.6 us (5%)
  other arithmetic  4.85 us (2%)
    all_gather x1, waiting for transfers between devices, gathered(): full = lax.all_gather(pair, ('x', 'y', 'core'), axis=0, tiled=False)  108 us
    pallas_call x2, Pallas kernels, spatial(): pl.pallas_call(spatial_kernel, out_shape=jax.ShapeDtypeStruct((height, br...  25.6 us
    all_to_all x1, blocking collectives, local(): lax.all_to_all(done, FRAME_AXIS, split_axis=0, concat_axis=0, tiled=True)  25.5 us
    all_to_all x2, starting transfers between devices, local(): lax.all_to_all(normed, FRAME_AXIS, split_axis=0, concat_axis=0, tiled=True)  16.6 us
    all_to_all x2, waiting for transfers between devices, local(): lax.all_to_all(normed, FRAME_AXIS, split_axis=0, concat_axis=0, tiled=True)  14.8 us
    ppermute x2, starting transfers between devices, local(): low = lax.ppermute(both, ROW_AXIS, down)  14 us
    pallas_call x1, Pallas kernels, temporal(): pl.pallas_call(temporal_kernel, out_shape=jax.ShapeDtypeStruct((peers, 2,...  13.3 us
    ppermute x1, waiting for transfers between devices, gathered(): other = lax.ppermute(mine, ('zh', 'zl'), [(i, 7 - i) for i in range(8)])  7.8 us
  transfers between devices with their start and end apart: 8, of which 3 were waited for; matrix products, arithmetic and copies ran while one was open for 4% of the time, Pallas kernels for 10%

profile of v2, /device:TPU:96, one launch (start us, length us, event | category | flops | bytes accessed | tf_op | source)
XLA Modules:
  0.0 265.5 jit_solution(3057150550496276448)
XLA Ops:
  6.5 1.1 fusion
  7.7 3.2 %collective-permute-start.2 = (bf16[72,1152]{1,0:T(8,128)(2,1)S(1)}, bf16[72,1152]{1,0:T(8,128)(2,1)S(1)}, u32[]{:S(2)}, u32[]{:S(2)}) collective-permute-start(bf16[72,1152]{1,0:T(8,128)(2,1)S(1)} %fusion), channel_id=1, source_target_pairs={{0,35},{1,34},{2,33},{3,32},{32,3},{33,2},{34,1},{35,0},{4,39},{5,... | collective-permute-start | bytes 497672 | tf_op jit(solution)/shard_map/ppermute | solution.py:285
  10.9 7.8 %collective-permute-done.2 = bf16[72,1152]{1,0:T(8,128)(2,1)S(1)} collective-permute-done((bf16[72,1152]{1,0:T(8,128)(2,1)S(1)}, bf16[72,1152]{1,0:T(8,128)(2,1)S(1)}, u32[]{:S(2)}, u32[]{:S(2)}) %collective-permute-start.2) | collective-permute-done | bytes 165920 | tf_op jit(solution)/shard_map/ppermute | solution.py:285
  18.7 0.8 pad_maximum_fusion.2
  19.5 0.0 all-gather.3.cloned.1.call-update
  19.6 0.2 fusion.7
  19.8 1.1 pad_maximum_fusion
  20.9 5.8 %collective-permute-start = (bf16[2,8,32,1152]{3,2,1,0:T(8,128)(2,1)}, bf16[2,8,32,1152]{3,2,1,0:T(8,128)(2,1)}, u32[]{:S(2)}, u32[]{:S(2)}) collective-permute-start(bf16[2,8,32,1152]{3,2,1,0:T(8,128)(2,1)} %pad_maximum_fusion), channel_id=1, source_target_pairs={{0,1},{1,2},{3,4},{4,5},{5,6},{7,8},{8,9},{9,10},{11,12},{12,13},{... | collective-permute-start | bytes 3538952 | tf_op jit(solution)/shard_map/ppermute | solution.py:315
  26.7 1.3 collective-permute-start.1
  28.0 0.0 copy-start.7
  28.1 1.1 pad_maximum_fusion.1
  29.2 8.3 %collective-permute-start.3 = (bf16[2,8,32,1152]{3,2,1,0:T(8,128)(2,1)}, bf16[2,8,32,1152]{3,2,1,0:T(8,128)(2,1)}, u32[]{:S(2)}, u32[]{:S(2)}) collective-permute-start(bf16[2,8,32,1152]{3,2,1,0:T(8,128)(2,1)} %pad_maximum_fusion.1), channel_id=1, source_target_pairs={{0,1},{1,2},{3,4},{4,5},{5,6},{7,8},{8,9},{9,10},{11,12},{12,13},{... | collective-permute-start | bytes 3538952 | tf_op jit(solution)/shard_map/ppermute | solution.py:315
  37.5 1.3 collective-permute-start.4
  38.8 0.6 fusion.9
  39.4 0.7 reshape.29.ids
  40.1 0.6 reshape.31.shift_ref
  40.7 0.6 reshape.32.scale_ref
  41.3 108.2 %all-gather.3.cloned.1.call-done = bf16[64,72,1152]{2,1,0:T(8,128)(2,1)} async-done(((bf16[2,72,1152]{2,1,0:T(8,128)(2,1)}), bf16[64,72,1152]{2,1,0:T(8,128)(2,1)}) %all-gather.3.cloned.1.call-update) | async-done | bytes 10616848 | tf_op jit(solution)/shard_map/all_gather | solution.py:288
  149.5 1.7 slice-done
  151.2 1.8 copy.17
  153.0 12.8 %spatial.2 = bf16[8,32,1152]{2,1,0:T(8,128)(2,1)} custom-call(s32[24]{0:T(128)} %reshape.29.ids, bf16[2,8,32,1152]{3,2,1,0:T(8,128)(2,1)} %q_ref.3, bf16[2,8,32,1152]{3,2,1,0:T(8,128)(2,1)} %k_own.3, bf16[2,8,32,1152]{3,2,1,0:T(8,128)(2,1)} %v_own.3, bf16[2,8,32,1152]{3,2,1,0:T(8,128)(2,1)} %collective-permute-done.low, ...), custom_call_target="tpu_custom_call" | custom-call | tf_op jit(solution)/shard_map/spatial/pallas_call | solution.py:172
  165.9 7.0 %all-to-all-start = ((bf16[16,16,1152]{2,1,0:T(8,128)(2,1)}), bf16[16,16,1152]{2,1,0:T(8,128)(2,1)}, u32[]{:S(2)}, u32[]{:S(2)}) async-start(bf16[16,16,1152]{2,1,0:T(8,128)(2,1)} %bitcast.24), calls=%async_computation | async-start | bytes 1179648 | tf_op jit(solution)/shard_map/all_to_all | solution.py:346
  172.9 3.3 %slice-done.1 = bf16[48,72,1152]{2,1,0:T(8,128)(2,1)S(1)} async-done(((bf16[64,72,1152]{2,1,0:T(8,128)(2,1)}), bf16[48,72,1152]{2,1,0:T(8,128)(2,1)S(1)}, s32[]{:S(2)}) %slice-start.1) | async-done | bytes 7962648 | tf_op jit(solution)/shard_map/slice | solution.py:290
  176.2 3.7 %copy.18 = bf16[3,4,2,2,72,1152]{5,4,2,3,1,0:T(8,128)(2,1)} copy(bf16[3,4,2,2,72,1152]{5,4,3,2,1,0:T(8,128)(2,1)S(1)} %bitcast.20) | data formatting | bytes 15925248 | tf_op jit(solution)/shard_map/slice | solution.py:290
  180.0 12.8 %spatial.3 = bf16[8,32,1152]{2,1,0:T(8,128)(2,1)} custom-call(s32[24]{0:T(128)} %reshape.29.ids, bf16[2,8,32,1152]{3,2,1,0:T(8,128)(2,1)} %q_ref.3, bf16[2,8,32,1152]{3,2,1,0:T(8,128)(2,1)} %k_own.3, bf16[2,8,32,1152]{3,2,1,0:T(8,128)(2,1)} %v_own.3, bf16[2,8,32,1152]{3,2,1,0:T(8,128)(2,1)} %collective-permute-done.3.low, ...), custom_call_target="tpu_custom_call" | custom-call | tf_op jit(solution)/shard_map/spatial/pallas_call | solution.py:172
  192.8 9.6 %all-to-all-start.1 = ((bf16[16,16,1152]{2,1,0:T(8,128)(2,1)}), bf16[16,16,1152]{2,1,0:T(8,128)(2,1)S(1)}, u32[]{:S(2)}, u32[]{:S(2)}) async-start(bf16[16,16,1152]{2,1,0:T(8,128)(2,1)} %bitcast.25), calls=%async_computation.1 | async-start | bytes 1179648 | tf_op jit(solution)/shard_map/all_to_all | solution.py:346
  202.4 0.6 convert_element_type.3.mask_ref
  203.0 14.8 %all-to-all-done.1 = bf16[16,16,1152]{2,1,0:T(8,128)(2,1)S(1)} async-done(((bf16[16,16,1152]{2,1,0:T(8,128)(2,1)}), bf16[16,16,1152]{2,1,0:T(8,128)(2,1)S(1)}, u32[]{:S(2)}, u32[]{:S(2)}) %all-to-all-start.1) | async-done | bytes 589856 | tf_op jit(solution)/shard_map/all_to_all | solution.py:346
  217.9 0.9 copy-done.2
  218.8 13.3 %temporal.1 = bf16[16,2,16,1152]{3,2,1,0:T(8,128)(2,1)} custom-call(bf16[256,1152]{1,0:T(8,128)(2,1)} %bitcast.6.even_ref, bf16[256,1152]{1,0:T(8,128)(2,1)} %bitcast.26, bf16[3,1152,1152]{2,1,0:T(8,128)(2,1)} %bitcast.18, bf16[8,8]{1,0:T(8,128)(2,1)} %convert_element_type.3.mask_ref), custom_call_target="tpu_custom_call" | custom-call | tf_op jit(solution)/shard_map/temporal/pallas_call | solution.py:256
  232.0 25.5 %all_to_all.27 = bf16[16,2,16,1152]{3,2,1,0:T(8,128)(2,1)S(1)} all-to-all(bf16[16,2,16,1152]{3,2,1,0:T(8,128)(2,1)} %temporal.1), channel_id=1, replica_groups=mesh['y'=4,'zh'=2,'core'=2,'x'=4,'zl'=4] {'y','zh','core'}, dimensions={0} | all-to-all | bytes 2359296 | tf_op jit(solution)/shard_map/all_to_all | solution.py:350
  257.5 1.1 copy.19
  (24 shorter events, 0.1 us)
Async XLA Ops:
  6.5 143.0 %all-gather.3.cloned.1.call-start = ((), (), s32[]{:S(2)}) async-start(), calls=%async_computation.3 | async-start | bytes 10948608 | tf_op jit(solution)/shard_map/all_gather | solution.py:288
  6.5 13.0 %copy-start = (bf16[2,8,32,1152]{3,2,1,0:T(8,128)(2,1)S(1)}, bf16[2,8,32,1152]{3,2,1,0:T(8,128)(2,1)}, u32[]{:S(2)}) copy-start(bf16[2,8,32,1152]{3,2,1,0:T(8,128)(2,1)} %k_own.3) | copy-start | bytes 3538948
  6.5 13.0 %copy-start.1 = (bf16[2,8,32,1152]{3,2,1,0:T(8,128)(2,1)S(1)}, bf16[2,8,32,1152]{3,2,1,0:T(8,128)(2,1)}, u32[]{:S(2)}) copy-start(bf16[2,8,32,1152]{3,2,1,0:T(8,128)(2,1)} %v_own.3) | copy-start | bytes 3538948
  7.7 11.0 %collective-permute-start.2 = (bf16[72,1152]{1,0:T(8,128)(2,1)S(1)}, bf16[72,1152]{1,0:T(8,128)(2,1)S(1)}, u32[]{:S(2)}, u32[]{:S(2)}) collective-permute-start(bf16[72,1152]{1,0:T(8,128)(2,1)S(1)} %fusion), channel_id=1, source_target_pairs={{0,35},{1,34},{2,33},{3,32},{32,3},{33,2},{34,1},{35,0},{4,39},{5,... | collective-permute-start | bytes 497672 | tf_op jit(solution)/shard_map/ppermute | solution.py:285
  20.9 132.1 %collective-permute-start = (bf16[2,8,32,1152]{3,2,1,0:T(8,128)(2,1)}, bf16[2,8,32,1152]{3,2,1,0:T(8,128)(2,1)}, u32[]{:S(2)}, u32[]{:S(2)}) collective-permute-start(bf16[2,8,32,1152]{3,2,1,0:T(8,128)(2,1)} %pad_maximum_fusion), channel_id=1, source_target_pairs={{0,1},{1,2},{3,4},{4,5},{5,6},{7,8},{8,9},{9,10},{11,12},{12,13},{... | collective-permute-start | bytes 3538952 | tf_op jit(solution)/shard_map/ppermute | solution.py:315
  26.7 126.3 %collective-permute-start.1 = (bf16[2,8,32,1152]{3,2,1,0:T(8,128)(2,1)}, bf16[2,8,32,1152]{3,2,1,0:T(8,128)(2,1)}, u32[]{:S(2)}, u32[]{:S(2)}) collective-permute-start(bf16[2,8,32,1152]{3,2,1,0:T(8,128)(2,1)} %pad_maximum_fusion), channel_id=1, source_target_pairs={{1,0},{2,1},{4,3},{5,4},{6,5},{8,7},{9,8},{10,9},{12,11},{13,12},{... | collective-permute-start | bytes 3538952 | tf_op jit(solution)/shard_map/ppermute | solution.py:316
  28.0 10.8 %copy-start.3 = (f32[2,1152]{1,0:T(2,128)S(1)}, f32[2,1152]{1,0:T(2,128)}, u32[]{:S(2)}) copy-start(f32[2,1152]{1,0:T(2,128)} %param.19) | copy-start | bytes 27652
  28.0 11.4 %copy-start.7 = (s32[4,6]{1,0:T(4,128)S(1)}, s32[4,6]{1,0:T(4,128)}, u32[]{:S(2)}) copy-start(s32[4,6]{1,0:T(4,128)} %param.15) | copy-start | bytes 292
  28.1 12.0 %copy-start.4 = (f32[1152]{0:T(1024)S(1)}, f32[1152]{0:T(1024)}, u32[]{:S(2)}) copy-start(f32[1152]{0:T(1024)} %param.20) | copy-start | bytes 13828
  28.1 12.6 %copy-start.5 = (f32[1152]{0:T(1024)S(1)}, f32[1152]{0:T(1024)}, u32[]{:S(2)}) copy-start(f32[1152]{0:T(1024)} %param.21) | copy-start | bytes 13828
  29.2 150.8 %collective-permute-start.3 = (bf16[2,8,32,1152]{3,2,1,0:T(8,128)(2,1)}, bf16[2,8,32,1152]{3,2,1,0:T(8,128)(2,1)}, u32[]{:S(2)}, u32[]{:S(2)}) collective-permute-start(bf16[2,8,32,1152]{3,2,1,0:T(8,128)(2,1)} %pad_maximum_fusion.1), channel_id=1, source_target_pairs={{0,1},{1,2},{3,4},{4,5},{5,6},{7,8},{8,9},{9,10},{11,12},{12,13},{... | collective-permute-start | bytes 3538952 | tf_op jit(solution)/shard_map/ppermute | solution.py:315
  37.5 142.5 %collective-permute-start.4 = (bf16[2,8,32,1152]{3,2,1,0:T(8,128)(2,1)}, bf16[2,8,32,1152]{3,2,1,0:T(8,128)(2,1)}, u32[]{:S(2)}, u32[]{:S(2)}) collective-permute-start(bf16[2,8,32,1152]{3,2,1,0:T(8,128)(2,1)} %pad_maximum_fusion.1), channel_id=1, source_target_pairs={{1,0},{2,1},{4,3},{5,4},{6,5},{8,7},{9,8},{10,9},{12,11},{13,12},{... | collective-permute-start | bytes 3538952 | tf_op jit(solution)/shard_map/ppermute | solution.py:316
  149.5 1.7 slice-start
  165.9 27.0 %all-to-all-start = ((bf16[16,16,1152]{2,1,0:T(8,128)(2,1)}), bf16[16,16,1152]{2,1,0:T(8,128)(2,1)}, u32[]{:S(2)}, u32[]{:S(2)}) async-start(bf16[16,16,1152]{2,1,0:T(8,128)(2,1)} %bitcast.24), calls=%async_computation | async-start | bytes 1179648 | tf_op jit(solution)/shard_map/all_to_all | solution.py:346
  172.9 3.3 %slice-start.1 = ((bf16[64,72,1152]{2,1,0:T(8,128)(2,1)}), bf16[48,72,1152]{2,1,0:T(8,128)(2,1)S(1)}, s32[]{:S(2)}) async-start(bf16[64,72,1152]{2,1,0:T(8,128)(2,1)} %all-gather.3.cloned.1.call-done), calls=%async_computation.5 | async-start | bytes 15925248 | tf_op jit(solution)/shard_map/slice | solution.py:290
  192.8 9.6 %copy-start.6 = (s32[8,8]{1,0:T(8,128)S(1)}, s32[8,8]{1,0:T(8,128)}, u32[]{:S(2)}) copy-start(s32[8,8]{1,0:T(8,128)} %param.16) | copy-start | bytes 772
  192.8 25.0 %all-to-all-start.1 = ((bf16[16,16,1152]{2,1,0:T(8,128)(2,1)}), bf16[16,16,1152]{2,1,0:T(8,128)(2,1)S(1)}, u32[]{:S(2)}, u32[]{:S(2)}) async-start(bf16[16,16,1152]{2,1,0:T(8,128)(2,1)} %bitcast.25), calls=%async_computation.1 | async-start | bytes 1179648 | tf_op jit(solution)/shard_map/all_to_all | solution.py:346
  217.9 0.9 copy-start.2
Sparse Core Ops, SparseCore 0:
  19.7 129.7 all-gather.2
